TPU v7x, 32 devices: a whole 2x2x4 slice. The times are simulated.
32 devices in a mesh: groups: 2 (over x), hist: 8 (over z, y), cand: 2 (over core).
Axes of the slice: x: 2, y: 2, z: 4, core: 2. Of those that a mesh axis runs over, the one named last changes fastest.
Arguments:
- candidates: bfloat16 [16, 1024, 512], P(('groups', 'hist'), 'cand'), parts along dimension 0, may hold values from -6 to 6
- hist_keys: bfloat16 [16, 1024, 512], P('groups', ('hist', 'cand')), parts along dimension 0, may hold values from -10 to 10
- hist_values: bfloat16 [16, 1024, 512], P('groups', ('hist', 'cand')), parts along dimension 0, may hold values from -6 to 6
- block_mask: int32 [16, 8, 8], P(('groups', 'hist')), parts along dimension 0, may hold values 0 or 1
- hist_blocks: int32 [16], P(('groups', 'hist')), parts along dimension 0, may hold values from 1 to 8, as said below
- proj_weight: bfloat16 [512, 1024], replicated, may hold values from -0.25 to 0.25
- out_weight: bfloat16 [512, 512], replicated, may hold values from -0.25 to 0.25
Outputs:
- cand_out: bfloat16 [16, 1024, 512], P(('groups', 'hist'), 'cand'), parts along dimension 0
There are 2 independent parts, one for each index of `groups`. A program takes and returns all parts, laid end to end along the dimension named above; an argument that names none is the same for every part. Nothing has to cross between parts.
Inputs may be any that keep to these rules, and one draw needn't show every extreme that they name: `hist_blocks`: some user has all 8 blocks.
All inputs are finite; a program needn't handle non-finite values. No bound on the sum of `block_mask` on one device may be relied on, other than what follows from the above.
Results may differ from a plain program's by a relative error of at most 0.013.
Values may be sent and summed in bfloat16 or wider, within the bound.
A program may use at most 64 MiB of HBM per device.

v0:
```python
import jax
import jax.numpy as jnp
from jax import lax
from jax.sharding import PartitionSpec as P

HEADS = 8
BLK = 128
EPS = 1e-05


def layer_norm(values_in):
    center = values_in - jnp.mean(values_in, axis=-1, keepdims=True)
    spread = jnp.mean(center * center, axis=-1, keepdims=True)
    return center * lax.rsqrt(spread + EPS)


def attend(running, query_heads, mask_rows, key_piece, value_piece, slab_count, group_rows, stride):
    piece_width = key_piece.shape[1]
    query_count = query_heads.shape[0]
    head_count = query_heads.shape[1]
    head_size = query_heads.shape[2]
    block_count = mask_rows.shape[0]
    block_total = mask_rows.shape[1]
    slab_keys = group_rows * piece_width
    score_scale = head_size ** (-0.5)

    def add_slab(slab_index, summed):
        key_slab = lax.dynamic_slice_in_dim(key_piece, slab_index * group_rows, group_rows, 0)
        value_slab = lax.dynamic_slice_in_dim(value_piece, slab_index * group_rows, group_rows, 0)
        key_slab = key_slab.reshape(slab_keys, head_count, head_size)
        value_slab = value_slab.reshape(slab_keys, head_count, head_size)
        positions = (slab_index * group_rows + jnp.arange(group_rows, dtype=jnp.int32))[
            :, None
        ] * stride
        positions = (positions + jnp.arange(piece_width, dtype=jnp.int32)[None, :]).reshape(
            slab_keys
        )
        onehot = (
            positions[None, :] // BLK == jnp.arange(block_total, dtype=jnp.int32)[:, None]
        ).astype(jnp.float32)
        key_mask = jnp.dot(mask_rows, onehot, preferred_element_type=jnp.float32)
        scores = (
            jnp.einsum("qhd,khd->hqk", query_heads, key_slab, preferred_element_type=jnp.float32)
            * score_scale
        )
        gated_scores = (
            jax.nn.silu(scores).reshape(head_count, block_count, BLK, slab_keys)
            * key_mask[None, :, None, :]
        )
        weights = gated_scores.reshape(head_count, query_count, slab_keys).astype(jnp.bfloat16)
        return summed + jnp.einsum(
            "hqk,khd->qhd", weights, value_slab, preferred_element_type=jnp.float32
        )

    return lax.fori_loop(0, slab_count, add_slab, running)


def on_device(candidates, hist_keys, hist_values, block_mask, hist_blocks, proj_weight, out_weight):
    cand_rows = candidates[0]
    own_count = cand_rows.shape[0]
    width_model = cand_rows.shape[1]
    head_count = HEADS
    head_size = width_model // head_count
    normed = layer_norm(cand_rows.astype(jnp.float32)).astype(jnp.bfloat16)
    projected = jax.nn.silu(
        jnp.dot(normed, proj_weight, preferred_element_type=jnp.float32)
    ).astype(jnp.bfloat16)
    gate_rows = projected[:, :width_model]
    queries = projected[:, width_model:]
    query_heads = queries.reshape(own_count, head_count, head_size)
    block_total = block_mask.shape[2]
    live_blocks = (jnp.arange(block_total, dtype=jnp.int32) < hist_blocks[0]).astype(jnp.float32)
    mask_eff = block_mask[0].astype(jnp.float32) * live_blocks[None, :]
    arrived_keys, arrived_values = (
        lax.all_to_all(hist_keys[:, None], "hist", split_axis=0, concat_axis=1, tiled=True),
        lax.all_to_all(hist_values[:, None], "hist", split_axis=0, concat_axis=1, tiled=True),
    )
    key_rows = arrived_keys[0]
    value_rows = arrived_values[0]
    hist_count = lax.axis_size("hist")
    cand_count = lax.axis_size("cand")
    cand_index = lax.axis_index("cand")
    per_device = key_rows.shape[1]
    stride = cand_count * per_device
    group_rows = min(8, hist_count)
    slab_count = hist_count // group_rows
    own_blocks = own_count // BLK
    own_mask = lax.dynamic_slice_in_dim(mask_eff, cand_index * own_blocks, own_blocks, 0)
    empty = jnp.zeros((own_count, head_count, head_size), jnp.float32)
    attended = attend(
        empty,
        query_heads,
        own_mask,
        lax.all_gather(key_rows, "cand", axis=1, tiled=True),
        lax.all_gather(value_rows, "cand", axis=1, tiled=True),
        slab_count,
        group_rows,
        stride,
    )
    attended = attended.reshape(own_count, width_model)
    mixed = (layer_norm(attended) * gate_rows.astype(jnp.float32)).astype(jnp.bfloat16)
    result = cand_rows.astype(jnp.float32) + jnp.dot(
        mixed, out_weight, preferred_element_type=jnp.float32
    )
    return result.astype(jnp.bfloat16)[None]


def solution(mesh):
    in_specs = (
        P(("groups", "hist"), "cand", None),
        P("groups", ("hist", "cand"), None),
        P("groups", ("hist", "cand"), None),
        P(("groups", "hist"), None, None),
        P(("groups", "hist")),
        P(),
        P(),
    )
    out_specs = P(("groups", "hist"), "cand", None)
    return jax.shard_map(
        on_device, mesh=mesh, in_specs=in_specs, out_specs=out_specs, check_vma=False
    )
```

profile of v0, /device:TPU:0, one launch (start us, length us, event | category | flops | bytes accessed | tf_op | source)
XLA Modules:
  0.0 81.3 jit_solution(10235428924594484104)
XLA Ops:
  6.5 22.1 %all_to_all.8 = bf16[8,1,64,512]{3,2,1,0:T(8,128)(2,1)} all-to-all(bf16[8,1,64,512]{3,2,1,0:T(8,128)(2,1)} %bitcast.74), channel_id=1, replica_groups=mesh['groups'=2,'hist'=8,'cand'=2] {'hist'}, dimensions={0} | all-to-all | bytes 1048576 | tf_op jit(solution)/shard_map/all_to_all | solution.py:75
  28.6 0.0 all-gather.5.cloned.1.call-update
  28.6 3.6 %all-to-all-start.1 = ((bf16[8,1,64,512]{3,2,1,0:T(8,128)(2,1)}), bf16[8,1,64,512]{3,2,1,0:T(8,128)(2,1)S(1)}, u32[]{:S(2)}, u32[]{:S(2)}) async-start(bf16[8,1,64,512]{3,2,1,0:T(8,128)(2,1)} %bitcast.75), calls=%async_computation.1 | async-start | bytes 1048576 | tf_op jit(solution)/shard_map/all_to_all | solution.py:76
  32.2 0.0 all-gather.7.cloned.1.call-start
  32.3 0.1 convert_reduce_fusion
  32.5 0.3 fusion.6
  32.8 13.6 %all-to-all-done.1 = bf16[8,1,64,512]{3,2,1,0:T(8,128)(2,1)S(1)} async-done(((bf16[8,1,64,512]{3,2,1,0:T(8,128)(2,1)}), bf16[8,1,64,512]{3,2,1,0:T(8,128)(2,1)S(1)}, u32[]{:S(2)}, u32[]{:S(2)}) %all-to-all-start.1) | async-done | bytes 524320 | tf_op jit(solution)/shard_map/all_to_all | solution.py:76
  46.4 0.8 copy-done.2
  47.2 0.0 all-gather.7.cloned.1.call-update
  47.3 1.0 %multiply_convert_fusion.1 = bf16[512,1024]{1,0:T(8,128)(2,1)S(1)} fusion(bf16[512,1024]{1,0:T(8,128)(2,1)S(1)} %copy-done, bf16[1,512,512]{2,1,0:T(8,128)(2,1)S(1)} %copy-done.1, f32[512]{0:T(512)S(1)} %add_rsqrt_fusion.1, f32[512]{0:T(512)S(1)} %broadcast_multiply_fusion.1), kind=kOutput, calls=%fused_computation.1 | convolution fusion | flops 540540928 | bytes 2625536 | tf_op jit(solution)/shard_map/dot_general | solution.py:66
  48.3 0.0 copy-start.6
  49.1 1.0 %copy.16 = bf16[512,512]{0,1:T(8,128)(2,1)} copy(bf16[512,512]{1,0:T(8,128)(2,1)S(1)} %slice.8) | data formatting | bytes 1048576 | tf_op jit(solution)/shard_map/slice | solution.py:69
  50.1 0.1 add_select_fusion
  50.2 0.1 fusion.19
  50.3 1.7 %copy.17 = bf16[8,1,128,512]{2,0,3,1:T(8,128)(2,1)S(1)} copy(bf16[8,1,128,512]{3,2,1,0:T(8,128)(2,1)} %all-gather.5.cloned.1.call-done) | data formatting | bytes 2097152 | tf_op jit(solution)/shard_map/all_gather | solution.py:94
  52.0 1.3 %reshape.148 = bf16[1024,8,64]{0,2,1:T(8,128)(2,1)} reshape(bf16[8,1,128,512]{2,0,3,1:T(8,128)(2,1)S(1)} %copy.17) | data formatting | bytes 2097152 | tf_op jit(solution)/shard_map/while/body/eval_jaxpr/reshape | solution.py:30
  53.3 2.2 %all-gather.7.cloned.1.call-done = bf16[8,1,128,512]{3,2,1,0:T(8,128)(2,1)} async-done(((bf16[8,1,64,512]{3,2,1,0:T(8,128)(2,1)}), bf16[8,1,128,512]{3,2,1,0:T(8,128)(2,1)}) %all-gather.7.cloned.1.call-update) | async-done | bytes 1048592 | tf_op jit(solution)/shard_map/all_gather | solution.py:95
  55.5 1.7 %copy.18 = bf16[8,1,128,512]{2,0,3,1:T(8,128)(2,1)S(1)} copy(bf16[8,1,128,512]{3,2,1,0:T(8,128)(2,1)} %all-gather.7.cloned.1.call-done) | data formatting | bytes 2097152 | tf_op jit(solution)/shard_map/all_gather | solution.py:95
  57.2 1.3 %reshape.149 = bf16[1024,8,64]{0,2,1:T(8,128)(2,1)} reshape(bf16[8,1,128,512]{2,0,3,1:T(8,128)(2,1)S(1)} %copy.18) | data formatting | bytes 2097152 | tf_op jit(solution)/shard_map/while/body/eval_jaxpr/reshape | solution.py:31
  58.5 1.6 %mul.90 = f32[4,128,1024]{2,1,0:T(8,128)} broadcast(f32[4,1024]{1,0:T(4,128)S(1)} %fusion.19), dimensions={0,2} | broadcast | bytes 2113536 | tf_op jit(solution)/shard_map/while/body/eval_jaxpr/mul | solution.py:47
  60.1 10.2 %fusion.28 = (f32[512]{0:T(512)S(1)}, f32[8,512,64]{1,2,0:T(8,128)S(1)}) fusion(bf16[1024,8,64]{0,2,1:T(8,128)(2,1)} %reshape.149, bf16[512,8,64]{0,2,1:T(8,128)(2,1)S(1)} %bitcast.76, bf16[1024,8,64]{0,2,1:T(8,128)(2,1)} %reshape.148, f32[512,1024]{1,0:T(8,128)} %bitcast.73), kind=kOutput, calls=%fused_computation.47 | convolution fusion | flops 1103363584 | bytes 5769216 | tf_op jit(solution)/shard_map/while/body/eval_jaxpr/hqk,khd->qhd/dot_general | solution.py:51
  70.3 0.2 fusion.9
  70.5 1.3 %copy.19 = f32[512,512]{1,0:T(8,128)} copy(f32[512,512]{0,1:T(8,128)S(1)} %bitcast.72) | data formatting | bytes 2097152 | tf_op jit(solution)/shard_map/reshape | solution.py:100
  71.8 2.7 %fusion.5 = bf16[1,512,512]{2,1,0:T(8,128)(2,1)} fusion(bf16[512,512]{1,0:T(8,128)(2,1)S(1)} %copy-done.5, bf16[1,512,512]{2,1,0:T(8,128)(2,1)S(1)} %copy-done.1, f32[512,512]{1,0:T(8,128)} %copy.19, bf16[512,1024]{1,0:T(8,128)(2,1)} %copy-done.3, f32[512]{0:T(512)S(1)} %add_rsqrt_fusion, f32[512]{0:T(512)S(1)} %broadcast_multiply_fusion), kind=kOutput, calls=%fused_computation.10 | convolution fusion | flops 270532608 | bytes 3149824 | tf_op jit(solution)/shard_map/dot_general | solution.py:102
  (22 shorter events, 0.1 us)
Async XLA Ops:
  6.5 40.7 %copy-start = (bf16[512,1024]{1,0:T(8,128)(2,1)S(1)}, bf16[512,1024]{1,0:T(8,128)(2,1)}, u32[]{:S(2)}) copy-start(bf16[512,1024]{1,0:T(8,128)(2,1)} %param.12) | copy-start | bytes 3145732
  6.5 25.8 %copy-start.1 = (bf16[1,512,512]{2,1,0:T(8,128)(2,1)S(1)}, bf16[1,512,512]{2,1,0:T(8,128)(2,1)}, u32[]{:S(2)}) copy-start(bf16[1,512,512]{2,1,0:T(8,128)(2,1)} %param.7) | copy-start | bytes 1572868
  6.5 43.8 %all-gather.5.cloned.1.call-start = ((), (), s32[]{:S(2)}) async-start(), calls=%async_computation.2 | async-start | bytes 1572864 | tf_op jit(solution)/shard_map/all_gather | solution.py:94
  28.6 17.8 %all-to-all-start.1 = ((bf16[8,1,64,512]{3,2,1,0:T(8,128)(2,1)}), bf16[8,1,64,512]{3,2,1,0:T(8,128)(2,1)S(1)}, u32[]{:S(2)}, u32[]{:S(2)}) async-start(bf16[8,1,64,512]{3,2,1,0:T(8,128)(2,1)} %bitcast.75), calls=%async_computation.1 | async-start | bytes 1048576 | tf_op jit(solution)/shard_map/all_to_all | solution.py:76
  32.2 23.2 %all-gather.7.cloned.1.call-start = ((), (), s32[]{:S(2)}) async-start(), calls=%async_computation.3 | async-start | bytes 1572864 | tf_op jit(solution)/shard_map/all_gather | solution.py:95
  46.4 0.8 copy-start.2
  48.3 2.0 %copy-start.3 = (bf16[512,1024]{1,0:T(8,128)(2,1)}, bf16[512,1024]{1,0:T(8,128)(2,1)S(1)}, u32[]{:S(2)}) copy-start(bf16[512,1024]{1,0:T(8,128)(2,1)S(1)} %multiply_convert_fusion.1) | copy-start | bytes 3145732
  48.3 1.9 %copy-start.6 = (s32[1,8,8]{2,1,0:T(8,128)S(1)}, s32[1,8,8]{2,1,0:T(8,128)}, u32[]{:S(2)}) copy-start(s32[1,8,8]{2,1,0:T(8,128)} %param.10) | copy-start | bytes 772
  57.2 2.9 %copy-start.4 = (bf16[512,512]{0,1:T(8,128)(2,1)S(1)}, bf16[512,512]{0,1:T(8,128)(2,1)}, u32[]{:S(2)}) copy-start(bf16[512,512]{0,1:T(8,128)(2,1)} %copy.16) | copy-start | bytes 1572868
  70.3 1.5 %copy-start.5 = (bf16[512,512]{1,0:T(8,128)(2,1)S(1)}, bf16[512,512]{1,0:T(8,128)(2,1)}, u32[]{:S(2)}) copy-start(bf16[512,512]{1,0:T(8,128)(2,1)} %param.13) | copy-start | bytes 1572868
Sparse Core Ops, SparseCore 0:
  28.8 8.0 all-gather.4
  47.4 8.0 all-gather.6
where the time goes:
time: 81.7 us; the launch traced here: 81.3 us
  blocking collectives  22.1 us (27%)
  waiting for transfers between devices  15.8 us (19%)
  between operations  14.2 us (17%)
  matrix products  14 us (17%)
  local copies, waits for them, and re-layouts  10.8 us (13%)
  starting transfers between devices  3.64 us (4%)
    all_to_all x1, blocking collectives, on_device(): lax.all_to_all(hist_keys[:, None], 'hist', split_axis=0, concat_axis=1, t...  22.1 us
    all_to_all x1, waiting for transfers between devices, on_device(): lax.all_to_all(hist_values[:, None], 'hist', split_axis=0, concat_axis=1,...  13.6 us
    dot_general x1, matrix products, add_slab(): jnp.einsum('hqk,khd->qhd', weights, value_slab, preferred_element_type=jn...  10.2 us
    all_to_all x1, starting transfers between devices, on_device(): lax.all_to_all(hist_values[:, None], 'hist', split_axis=0, concat_axis=1,...  3.61 us
    dot_general x1, matrix products, on_device(): jnp.dot(mixed, out_weight, preferred_element_type=jnp.float32)  2.66 us
    all_gather x1, waiting for transfers between devices, on_device(): lax.all_gather(value_rows, 'cand', axis=1, tiled=True)  2.16 us
    all_gather x1, local copies, waits for them, and re-layouts, on_device(): lax.all_gather(key_rows, 'cand', axis=1, tiled=True)  1.72 us
    all_gather x1, local copies, waits for them, and re-layouts, on_device(): lax.all_gather(value_rows, 'cand', axis=1, tiled=True)  1.71 us
  transfers between devices with their start and end apart: 3, of which 2 were waited for; matrix products, arithmetic and copies ran while one was open for 7% of the time, Pallas kernels for 0%

commit v1 on v0

--- a/solution.py
+++ b/solution.py
@@ -6,6 +6,13 @@
 HEADS = 8
 BLK = 128
 EPS = 1e-05
+
+
+def stacked_exchange(block, axis, split, join):
+    size = lax.axis_size(axis)
+    pieces = jnp.stack(jnp.split(block, size, axis=split), axis=0)
+    pieces = lax.all_to_all(pieces, axis, split_axis=0, concat_axis=0)
+    return jnp.concatenate(pieces, axis=join)
 
 
 def layer_norm(values_in):
@@ -72,7 +79,7 @@
     live_blocks = (jnp.arange(block_total, dtype=jnp.int32) < hist_blocks[0]).astype(jnp.float32)
     mask_eff = block_mask[0].astype(jnp.float32) * live_blocks[None, :]
     arrived_keys, arrived_values = (
-        lax.all_to_all(hist_keys[:, None], "hist", split_axis=0, concat_axis=1, tiled=True),
+        stacked_exchange(hist_keys[:, None], "hist", 0, 1),
         lax.all_to_all(hist_values[:, None], "hist", split_axis=0, concat_axis=1, tiled=True),
     )
     key_rows = arrived_keys[0]

time: 81.7 us -> 84.8 us (1.038)
  blocking collectives: 22.1 us -> 0 us
  local copies, waits for them, and re-layouts: 10.8 us -> 23.2 us
  starting transfers between devices: 3.64 us -> 11.1 us
  waiting for transfers between devices: 15.8 us -> 20.6 us
    all_to_all x1 -> x0, blocking collectives: 22.1 us -> none  [on_device(): lax.all_to_all(hist_keys[:, None], 'hist', split_axis=0, concat_axis=1, t...]
    all_to_all x0 -> x1, waiting for transfers between devices: none -> 14.1 us  [stacked_exchange(): pieces = lax.all_to_all(pieces, axis, split_axis=0, concat_axis=0)]
    unnamed x14 -> x23, local copies, waits for them, and re-layouts: 0.82 us -> 11.8 us
    all_to_all x1, waiting for transfers between devices: 13.6 us -> 4.22 us  [on_device(): lax.all_to_all(hist_values[:, None], 'hist', split_axis=0, concat_axis=1,...]
    all_to_all x1, starting transfers between devices: 3.61 us -> 7.44 us  [on_device(): lax.all_to_all(hist_values[:, None], 'hist', split_axis=0, concat_axis=1,...]
    all_to_all x0 -> x1, starting transfers between devices: none -> 3.64 us  [stacked_exchange(): pieces = lax.all_to_all(pieces, axis, split_axis=0, concat_axis=0)]
    all_gather x1, waiting for transfers between devices: 0.01 us -> 2.17 us  [on_device(): lax.all_gather(key_rows, 'cand', axis=1, tiled=True)]
    all_gather x1, waiting for transfers between devices: 2.16 us -> 0.01 us  [on_device(): lax.all_gather(value_rows, 'cand', axis=1, tiled=True)]
  transfers between devices with their start and end apart: 3 -> 4, of which waited for: 2 -> 3; matrix products, arithmetic and copies ran while one was open for 7% -> 21% of each run, Pallas kernels for 0% -> 0%
where the time goes in v1:
time: 84.8 us; the launch traced here: 84 us
  local copies, waits for them, and re-layouts  23.2 us (27%)
  waiting for transfers between devices  20.6 us (24%)
  between operations  14.3 us (17%)
  matrix products  14 us (17%)
  starting transfers between devices  11.1 us (13%)
    all_to_all x1, waiting for transfers between devices, stacked_exchange(): pieces = lax.all_to_all(pieces, axis, split_axis=0, concat_axis=0)  14.1 us
    unnamed x23, local copies, waits for them, and re-layouts  11.8 us
    dot_general x1, matrix products, add_slab(): jnp.einsum('hqk,khd->qhd', weights, value_slab, preferred_element_type=jn...  10.2 us
    all_to_all x1, starting transfers between devices, on_device(): lax.all_to_all(hist_values[:, None], 'hist', split_axis=0, concat_axis=1,...  7.44 us
    all_to_all x1, waiting for transfers between devices, on_device(): lax.all_to_all(hist_values[:, None], 'hist', split_axis=0, concat_axis=1,...  4.22 us
    all_to_all x1, starting transfers between devices, stacked_exchange(): pieces = lax.all_to_all(pieces, axis, split_axis=0, concat_axis=0)  3.64 us
    dot_general x1, matrix products, on_device(): jnp.dot(mixed, out_weight, preferred_element_type=jnp.float32)  2.66 us
    all_gather x1, waiting for transfers between devices, on_device(): lax.all_gather(key_rows, 'cand', axis=1, tiled=True)  2.17 us
  transfers between devices with their start and end apart: 4, of which 3 were waited for; matrix products, arithmetic and copies ran while one was open for 21% of the time, Pallas kernels for 0%

profile of v1, /device:TPU:0, one launch (start us, length us, event | category | flops | bytes accessed | tf_op | source)
XLA Modules:
  0.0 84.0 jit_solution(5717797832430615762)
XLA Ops:
  6.5 7.4 %all-to-all-start.1 = ((bf16[8,1,64,512]{3,2,1,0:T(8,128)(2,1)}), bf16[8,1,64,512]{3,2,1,0:T(8,128)(2,1)S(1)}, u32[]{:S(2)}, u32[]{:S(2)}) async-start(bf16[8,1,64,512]{3,2,1,0:T(8,128)(2,1)} %bitcast.89), calls=%async_computation.1 | async-start | bytes 1048576 | tf_op jit(solution)/shard_map/all_to_all | solution.py:83
  14.0 1.5 %bitcast_dynamic-update-slice_fusion.7 = bf16[8,1,1,64,512]{4,3,2,1,0:T(8,128)(2,1)} fusion(bf16[8,64,512]{2,1,0:T(8,128)(2,1)} %param.8), kind=kLoop, calls=%fused_computation.30 | loop fusion | bytes 131072
  15.5 1.5 %bitcast_dynamic-update-slice_fusion.6 = bf16[8,1,1,64,512]{4,3,2,1,0:T(8,128)(2,1)} fusion(bf16[8,1,1,64,512]{4,3,2,1,0:T(8,128)(2,1)} %bitcast_dynamic-update-slice_fusion.7, bf16[8,64,512]{2,1,0:T(8,128)(2,1)} %param.8), kind=kLoop, calls=%fused_computation.29 | loop fusion | bytes 131072
  16.9 1.5 %bitcast_dynamic-update-slice_fusion.5 = bf16[8,1,1,64,512]{4,3,2,1,0:T(8,128)(2,1)} fusion(bf16[8,1,1,64,512]{4,3,2,1,0:T(8,128)(2,1)} %bitcast_dynamic-update-slice_fusion.6, bf16[8,64,512]{2,1,0:T(8,128)(2,1)} %param.8), kind=kLoop, calls=%fused_computation.28 | loop fusion | bytes 131072
  18.4 1.5 %bitcast_dynamic-update-slice_fusion.4 = bf16[8,1,1,64,512]{4,3,2,1,0:T(8,128)(2,1)} fusion(bf16[8,1,1,64,512]{4,3,2,1,0:T(8,128)(2,1)} %bitcast_dynamic-update-slice_fusion.5, bf16[8,64,512]{2,1,0:T(8,128)(2,1)} %param.8), kind=kLoop, calls=%fused_computation.27 | loop fusion | bytes 131072
  19.9 1.5 %bitcast_dynamic-update-slice_fusion.3 = bf16[8,1,1,64,512]{4,3,2,1,0:T(8,128)(2,1)} fusion(bf16[8,1,1,64,512]{4,3,2,1,0:T(8,128)(2,1)} %bitcast_dynamic-update-slice_fusion.4, bf16[8,64,512]{2,1,0:T(8,128)(2,1)} %param.8), kind=kLoop, calls=%fused_computation.26 | loop fusion | bytes 131072
  21.3 1.5 %bitcast_dynamic-update-slice_fusion.2 = bf16[8,1,1,64,512]{4,3,2,1,0:T(8,128)(2,1)} fusion(bf16[8,1,1,64,512]{4,3,2,1,0:T(8,128)(2,1)} %bitcast_dynamic-update-slice_fusion.3, bf16[8,64,512]{2,1,0:T(8,128)(2,1)} %param.8), kind=kLoop, calls=%fused_computation.25 | loop fusion | bytes 131072
  22.8 1.5 %bitcast_dynamic-update-slice_fusion.1 = bf16[8,1,1,64,512]{4,3,2,1,0:T(8,128)(2,1)} fusion(bf16[8,1,1,64,512]{4,3,2,1,0:T(8,128)(2,1)} %bitcast_dynamic-update-slice_fusion.2, bf16[8,64,512]{2,1,0:T(8,128)(2,1)} %param.8), kind=kLoop, calls=%fused_computation.24 | loop fusion | bytes 131072
  24.2 4.2 %all-to-all-done.1 = bf16[8,1,64,512]{3,2,1,0:T(8,128)(2,1)S(1)} async-done(((bf16[8,1,64,512]{3,2,1,0:T(8,128)(2,1)}), bf16[8,1,64,512]{3,2,1,0:T(8,128)(2,1)S(1)}, u32[]{:S(2)}, u32[]{:S(2)}) %all-to-all-start.1) | async-done | bytes 524320 | tf_op jit(solution)/shard_map/all_to_all | solution.py:83
  29.3 1.5 %bitcast_dynamic-update-slice_fusion = bf16[8,1,1,64,512]{4,3,2,1,0:T(8,128)(2,1)} fusion(bf16[8,1,1,64,512]{4,3,2,1,0:T(8,128)(2,1)} %bitcast_dynamic-update-slice_fusion.1, bf16[8,64,512]{2,1,0:T(8,128)(2,1)} %param.8), kind=kLoop, calls=%fused_computation.23 | loop fusion | bytes 131072 | tf_op jit(solution)/shard_map/stack | solution.py:13
  30.8 3.6 %all-to-all-start = ((bf16[8,1,1,64,512]{4,3,2,1,0:T(8,128)(2,1)}), bf16[8,1,1,64,512]{4,3,2,1,0:T(8,128)(2,1)S(1)}, u32[]{:S(2)}, u32[]{:S(2)}) async-start(bf16[8,1,1,64,512]{4,3,2,1,0:T(8,128)(2,1)} %bitcast_dynamic-update-slice_fusion), calls=%async_computation | async-start | bytes 1048576 | tf_op jit(solution)/shard_map/all_to_all | solution.py:14
  34.9 14.1 %all-to-all-done = bf16[8,1,1,64,512]{4,3,2,1,0:T(8,128)(2,1)S(1)} async-done(((bf16[8,1,1,64,512]{4,3,2,1,0:T(8,128)(2,1)}), bf16[8,1,1,64,512]{4,3,2,1,0:T(8,128)(2,1)S(1)}, u32[]{:S(2)}, u32[]{:S(2)}) %all-to-all-start) | async-done | bytes 524320 | tf_op jit(solution)/shard_map/all_to_all | solution.py:14
  49.1 0.8 copy-done.3
  49.9 1.0 %multiply_convert_fusion.1 = bf16[512,1024]{1,0:T(8,128)(2,1)S(1)} fusion(bf16[512,1024]{1,0:T(8,128)(2,1)S(1)} %copy-done, bf16[1,512,512]{2,1,0:T(8,128)(2,1)S(1)} %copy-done.1, f32[512]{0:T(512)S(1)} %add_rsqrt_fusion.1, f32[512]{0:T(512)S(1)} %broadcast_multiply_fusion.1), kind=kOutput, calls=%fused_computation.1 | convolution fusion | flops 540540928 | bytes 2625536 | tf_op jit(solution)/shard_map/dot_general | solution.py:73
  51.7 1.0 %copy.16 = bf16[512,512]{0,1:T(8,128)(2,1)} copy(bf16[512,512]{1,0:T(8,128)(2,1)S(1)} %slice.16) | data formatting | bytes 1048576 | tf_op jit(solution)/shard_map/slice | solution.py:76
  53.0 1.7 %copy.18 = bf16[8,1,128,512]{2,0,3,1:T(8,128)(2,1)S(1)} copy(bf16[8,1,128,512]{3,2,1,0:T(8,128)(2,1)} %all-gather.7.cloned.1.call-done) | data formatting | bytes 2097152 | tf_op jit(solution)/shard_map/all_gather | solution.py:102
  54.7 1.3 %reshape.161 = bf16[1024,8,64]{0,2,1:T(8,128)(2,1)} reshape(bf16[8,1,128,512]{2,0,3,1:T(8,128)(2,1)S(1)} %copy.18) | data formatting | bytes 2097152 | tf_op jit(solution)/shard_map/while/body/eval_jaxpr/reshape | solution.py:38
  55.9 2.2 %all-gather.5.cloned.1.call-done = bf16[8,1,1,128,512]{4,3,2,1,0:T(8,128)(2,1)} async-done(((bf16[8,1,1,64,512]{4,3,2,1,0:T(8,128)(2,1)}), bf16[8,1,1,128,512]{4,3,2,1,0:T(8,128)(2,1)}) %all-gather.5.cloned.1.call-update) | async-done | bytes 1048592 | tf_op jit(solution)/shard_map/all_gather | solution.py:101
  58.1 1.7 %copy.17 = bf16[8,1,1,128,512]{3,0,4,2,1:T(8,128)(2,1)S(1)} copy(bf16[8,1,1,128,512]{4,3,2,1,0:T(8,128)(2,1)} %all-gather.5.cloned.1.call-done) | data formatting | bytes 2097152 | tf_op jit(solution)/shard_map/all_gather | solution.py:101
  59.8 1.3 %reshape.160 = bf16[1024,8,64]{0,2,1:T(8,128)(2,1)} reshape(bf16[8,1,1,128,512]{3,0,4,2,1:T(8,128)(2,1)S(1)} %copy.17) | data formatting | bytes 2097152 | tf_op jit(solution)/shard_map/while/body/eval_jaxpr/reshape | solution.py:37
  61.1 1.6 %mul.90 = f32[4,128,1024]{2,1,0:T(8,128)} broadcast(f32[4,1024]{1,0:T(4,128)S(1)} %fusion.19), dimensions={0,2} | broadcast | bytes 2113536 | tf_op jit(solution)/shard_map/while/body/eval_jaxpr/mul | solution.py:54
  62.7 10.2 %fusion.28 = (f32[512]{0:T(512)S(1)}, f32[8,512,64]{1,2,0:T(8,128)S(1)}) fusion(bf16[1024,8,64]{0,2,1:T(8,128)(2,1)} %reshape.161, bf16[512,8,64]{0,2,1:T(8,128)(2,1)S(1)} %bitcast.90, bf16[1024,8,64]{0,2,1:T(8,128)(2,1)} %reshape.160, f32[512,1024]{1,0:T(8,128)} %bitcast.88), kind=kOutput, calls=%fused_computation.55 | convolution fusion | flops 1103363584 | bytes 5769216 | tf_op jit(solution)/shard_map/while/body/eval_jaxpr/hqk,khd->qhd/dot_general | solution.py:58
  73.2 1.3 %copy.19 = f32[512,512]{1,0:T(8,128)} copy(f32[512,512]{0,1:T(8,128)S(1)} %bitcast.87) | data formatting | bytes 2097152 | tf_op jit(solution)/shard_map/reshape | solution.py:107
  74.5 2.7 %fusion.5 = bf16[1,512,512]{2,1,0:T(8,128)(2,1)} fusion(bf16[512,512]{1,0:T(8,128)(2,1)S(1)} %copy-done.6, bf16[1,512,512]{2,1,0:T(8,128)(2,1)S(1)} %copy-done.1, f32[512,512]{1,0:T(8,128)} %copy.19, bf16[512,1024]{1,0:T(8,128)(2,1)} %copy-done.4, f32[512]{0:T(512)S(1)} %add_rsqrt_fusion, f32[512]{0:T(512)S(1)} %broadcast_multiply_fusion), kind=kOutput, calls=%fused_computation.10 | convolution fusion | flops 270532608 | bytes 3149824 | tf_op jit(solution)/shard_map/dot_general | solution.py:109
  (33 shorter events, 1.8 us)
Async XLA Ops:
  6.5 43.4 %copy-start = (bf16[512,1024]{1,0:T(8,128)(2,1)S(1)}, bf16[512,1024]{1,0:T(8,128)(2,1)}, u32[]{:S(2)}) copy-start(bf16[512,1024]{1,0:T(8,128)(2,1)} %param.12) | copy-start | bytes 3145732
  6.5 27.9 %copy-start.1 = (bf16[1,512,512]{2,1,0:T(8,128)(2,1)S(1)}, bf16[1,512,512]{2,1,0:T(8,128)(2,1)}, u32[]{:S(2)}) copy-start(bf16[1,512,512]{2,1,0:T(8,128)(2,1)} %param.7) | copy-start | bytes 1572868
  6.5 21.9 %all-to-all-start.1 = ((bf16[8,1,64,512]{3,2,1,0:T(8,128)(2,1)}), bf16[8,1,64,512]{3,2,1,0:T(8,128)(2,1)S(1)}, u32[]{:S(2)}, u32[]{:S(2)}) async-start(bf16[8,1,64,512]{3,2,1,0:T(8,128)(2,1)} %bitcast.89), calls=%async_computation.1 | async-start | bytes 1048576 | tf_op jit(solution)/shard_map/all_to_all | solution.py:83
  14.0 39.0 %all-gather.7.cloned.1.call-start = ((), (), s32[]{:S(2)}) async-start(), calls=%async_computation.3 | async-start | bytes 1572864 | tf_op jit(solution)/shard_map/all_gather | solution.py:102
  28.5 0.8 copy-start.2
  30.8 18.3 %all-to-all-start = ((bf16[8,1,1,64,512]{4,3,2,1,0:T(8,128)(2,1)}), bf16[8,1,1,64,512]{4,3,2,1,0:T(8,128)(2,1)S(1)}, u32[]{:S(2)}, u32[]{:S(2)}) async-start(bf16[8,1,1,64,512]{4,3,2,1,0:T(8,128)(2,1)} %bitcast_dynamic-update-slice_fusion), calls=%async_computation | async-start | bytes 1048576 | tf_op jit(solution)/shard_map/all_to_all | solution.py:14
  34.4 23.7 %all-gather.5.cloned.1.call-start = ((), (), s32[]{:S(2)}) async-start(), calls=%async_computation.2 | async-start | bytes 1572864 | tf_op jit(solution)/shard_map/all_gather | solution.py:101
  49.1 0.8 copy-start.3
  50.9 2.0 %copy-start.4 = (bf16[512,1024]{1,0:T(8,128)(2,1)}, bf16[512,1024]{1,0:T(8,128)(2,1)S(1)}, u32[]{:S(2)}) copy-start(bf16[512,1024]{1,0:T(8,128)(2,1)S(1)} %multiply_convert_fusion.1) | copy-start | bytes 3145732
  50.9 1.9 %copy-start.7 = (s32[1,8,8]{2,1,0:T(8,128)S(1)}, s32[1,8,8]{2,1,0:T(8,128)}, u32[]{:S(2)}) copy-start(s32[1,8,8]{2,1,0:T(8,128)} %param.10) | copy-start | bytes 772
  59.8 2.9 %copy-start.5 = (bf16[512,512]{0,1:T(8,128)(2,1)S(1)}, bf16[512,512]{0,1:T(8,128)(2,1)}, u32[]{:S(2)}) copy-start(bf16[512,512]{0,1:T(8,128)(2,1)} %copy.16) | copy-start | bytes 1572868
  73.0 1.5 %copy-start.6 = (bf16[512,512]{1,0:T(8,128)(2,1)S(1)}, bf16[512,512]{1,0:T(8,128)(2,1)}, u32[]{:S(2)}) copy-start(bf16[512,512]{1,0:T(8,128)(2,1)} %param.13) | copy-start | bytes 1572868
Sparse Core Ops, SparseCore 0:
  29.4 8.0 all-gather.6
  50.0 8.0 all-gather.4
